TPU v7x, 32 devices: a whole 2x2x4 slice. The times are simulated.
32 devices in a mesh: tm: 16 (over z, y, x), row: 2 (over core).
Axes of the slice: x: 2, y: 2, z: 4, core: 2. Of those that a mesh axis runs over, the one named last changes fastest.
Arguments:
- initial: float32 [1024], replicated, may hold values from -6 to 6
- dynamics: float32 [1024, 1024], replicated, may hold values from -0.009765625 to 0.009765625
- obs_rows: bfloat16 [32768, 1024], P('tm', 'row'), may hold values from -0.1875 to 0.1875
- obs_values: bfloat16 [32768], P('tm'), may hold values from -6 to 6
- obs_slab: int32 [32768, 1], P('tm'), may hold values from 0 to 31; in each aligned block of 2048 rows (0 to 2047, 2048 to 4095, ...) at most 64 rows name the same one
Outputs:
- states: float32 [32, 1024], P('tm', 'row')
Inputs may be any that keep to these rules, and one draw needn't show every extreme that they name: `obs_slab`: within the rows ingested by one index of tm, no slab is named by more than 64 rows, a bound that some block reaches of them.
All inputs are finite; a program needn't handle non-finite values.
Results may differ from a plain program's by a relative error of at most 0.0003.
Values may be sent and summed in bfloat16 or wider, within the bound.
A program may use at most 128 MiB of HBM per device.

v0:
```python
import jax
import jax.numpy as jnp
from jax import lax
from jax.sharding import PartitionSpec as P

SLAB_DEV = 2
CAP = 64
sigma_gain = 0.3


def shifted(value, axis, steps):
    count = lax.axis_size(axis)
    first, last = (max(0, -steps), min(count, count - steps))
    return lax.ppermute(value, axis, [(source, source + steps) for source in range(first, last)])


def left_product(left_rows, pieces):
    new_matrix = jnp.dot(left_rows, pieces[0], precision=lax.Precision.HIGHEST)
    new_vector = jnp.dot(left_rows, pieces[1], precision=lax.Precision.HIGHEST)
    return (new_matrix, new_vector)


def body(initial, dynamics, obs_rows, obs_values, obs_slab):
    time_devs = lax.axis_size("tm")
    row_devs = lax.axis_size("row")
    state_width = dynamics.shape[1]
    local_cols = state_width // row_devs
    row_start = lax.axis_index("row") * local_cols
    time_index = lax.axis_index("tm")
    capacity = CAP
    slab_total = SLAB_DEV * time_devs
    obs_count = obs_rows.shape[0]
    target = obs_slab[:, 0]
    onehot = (target[:, None] == jnp.arange(slab_total, dtype=jnp.int32)[None, :]).astype(jnp.int32)
    rank_in = jnp.sum(onehot * (jnp.cumsum(onehot, axis=0) - 1), axis=1)
    owner_dev = target // SLAB_DEV
    within = target % SLAB_DEV
    slot_index = (within * time_devs + owner_dev) * capacity + rank_in
    slot_table = (
        jnp.full((slab_total * capacity,), obs_count, jnp.int32)
        .at[slot_index]
        .set(jnp.arange(obs_count, dtype=jnp.int32))
    )
    padded_rows = jnp.concatenate([obs_rows, jnp.zeros((1, local_cols), jnp.bfloat16)], axis=0)
    padded_values = jnp.concatenate([obs_values, jnp.zeros((1,), jnp.bfloat16)], axis=0)
    send_rows = padded_rows[slot_table].reshape(SLAB_DEV, time_devs, capacity, local_cols)
    send_values = padded_values[slot_table].reshape(SLAB_DEV, time_devs, capacity)
    recv_rows, recv_values = (
        lax.all_to_all(send_rows, "tm", split_axis=1, concat_axis=1, tiled=True),
        lax.all_to_all(send_values, "tm", split_axis=1, concat_axis=1, tiled=True),
    )
    slab_rows = recv_rows.reshape(SLAB_DEV, time_devs * capacity, local_cols)
    slab_values = recv_values.reshape(SLAB_DEV, time_devs * capacity)
    information = jnp.einsum(
        "sra,srb->sab",
        slab_rows,
        lax.all_gather(slab_rows, "row", axis=2, tiled=True),
        preferred_element_type=jnp.float32,
    )
    moment = jnp.einsum("sr,sra->sa", slab_values, slab_rows, preferred_element_type=jnp.float32)
    evolve = jnp.eye(state_width, dtype=jnp.float32) + dynamics
    evolve_rows = lax.dynamic_slice_in_dim(evolve, row_start, local_cols, 0)
    transitions = []
    offsets = []
    for slab_index in range(SLAB_DEV):
        transitions.append(
            evolve_rows
            - sigma_gain * jnp.dot(information[slab_index], evolve, precision=lax.Precision.HIGHEST)
        )
        offsets.append(sigma_gain * moment[slab_index])
    composed = transitions[0]
    composed_offset = offsets[0]
    slab_index = 1
    new_matrix, new_vector = left_product(
        transitions[slab_index],
        (
            lax.all_gather(composed, "row", axis=0, tiled=True),
            lax.all_gather(composed_offset, "row", axis=0, tiled=True),
        ),
    )
    composed = new_matrix
    composed_offset = new_vector + offsets[slab_index]
    initial_rows = lax.dynamic_slice_in_dim(initial, row_start, local_cols, 0)

    def advance(turn, state_rows):
        whole_state = lax.all_gather(state_rows, "row", axis=0, tiled=True)
        leaving = jnp.dot(composed, whole_state, precision=lax.Precision.HIGHEST) + composed_offset
        arriving = shifted(leaving, "tm", 1)
        return jnp.where(time_index == 0, initial_rows, arriving)

    entry_rows = lax.fori_loop(0, time_devs - 1, advance, initial_rows)
    states = []
    current = entry_rows
    for slab_index in range(SLAB_DEV):
        whole_state = lax.all_gather(current, "row", axis=0, tiled=True)
        current = (
            jnp.dot(transitions[slab_index], whole_state, precision=lax.Precision.HIGHEST)
            + offsets[slab_index]
        )
        states.append(current)
    return jnp.stack(states)


def solution(mesh):
    placed = (P(), P(), P("tm", "row"), P("tm"), P("tm", None))
    return jax.shard_map(
        body, mesh=mesh, in_specs=placed, out_specs=P("tm", "row"), check_vma=False
    )
```

profile of v0, /device:TPU:9, one launch (start us, length us, event | category | flops | bytes accessed | tf_op | source)
XLA Modules:
  0.0 357.0 jit_solution(5598932367776925572)
XLA Ops:
  7.3 9.1 %reduce-window.6 = s32[32,16,128]{2,1,0:T(8,128)S(1)} reduce-window(s32[32,16,128]{2,1,0:T(8,128)S(1)} %fusion.4, s32[]{:T(128)} %copy.37), window={size=1x1x128 pad=0_0x0_0x127_0}, to_apply=%region_0.0 | reduce-window | flops 8323072 | bytes 524292 | tf_op jit(solution)/shard_map/reduce-window
  17.3 8.0 %scatter_custom_fusion = s32[2048]{0:T(1024)S(1)} fusion(s32[2048]{0:T(1024)S(1)} %bitcast.110, s32[2048]{0:T(1024)S(1)} %iota.23, s32[]{:T(128)} %constant.63.clone.1), kind=kCustom, calls=%fused_computation.34 | custom fusion | bytes 8196 | tf_op jit(solution)/shard_map/scatter | solution.py:42
  27.1 9.2 %gather_fusion = bf16[2048,512]{1,0:T(8,128)(2,1)} fusion(bf16[2049,512]{1,0:T(8,128)(2,1)S(1)} %concatenate.6, s32[2048]{0:T(1024)S(1)} %fusion.5), kind=kCustom, calls=%fused_computation | custom fusion | bytes 4202496 | tf_op jit(solution)/shard_map/gather | solution.py:46
  38.2 53.8 %all_to_all.10 = bf16[2,16,64,512]{3,2,0,1:T(8,128)(2,1)S(1)} all-to-all(bf16[2,16,64,512]{3,2,0,1:T(8,128)(2,1)S(1)} %copy.17), channel_id=1, replica_groups=mesh['tm'=16,'row'=2] {'tm'}, dimensions={1} | all-to-all | bytes 4194304 | tf_op jit(solution)/shard_map/all_to_all | solution.py:49
  93.7 5.0 %convert_add_fusion = f32[1024,1024]{1,0:T(8,128)} fusion(f32[1024,1024]{1,0:T(8,128)} %param.8), kind=kLoop, calls=%fused_computation.4 | loop fusion | flops 3145728 | bytes 8388608 | tf_op jit(solution)/shard_map/add | solution.py:61
  98.6 9.4 %all-gather.9.cloned.1.call-done = bf16[2,1024,1024]{2,1,0:T(8,128)(2,1)} async-done(((bf16[2,1024,512]{2,1,0:T(8,128)(2,1)}), bf16[2,1024,1024]{2,1,0:T(8,128)(2,1)}) %all-gather.9.cloned.1.call-update) | async-done | bytes 4194320 | tf_op jit(solution)/shard_map/all_gather | solution.py:57
  108.0 4.7 %fusion.13 = f32[2,512,1024]{2,1,0:T(8,128)S(1)} fusion(bf16[2,1024,512]{2,1,0:T(8,128)(2,1)S(1)} %bitcast.86, bf16[2,1024,1024]{2,1,0:T(8,128)(2,1)} %all-gather.9.cloned.1.call-done), kind=kOutput, calls=%fused_computation.39 | convolution fusion | flops 2147483648 | bytes 10485760 | tf_op jit(solution)/shard_map/sra,srb->sab/dot_general | solution.py:54
  112.8 1.9 copy-done.4
  114.7 8.2 %multiply_subtract_fusion.1 = f32[512,1024]{1,0:T(8,128)} fusion(f32[1024,1024]{1,0:T(8,128)S(1)} %copy-done, s32[]{:T(128)S(6)} %select_n.38, f32[2,512,1024]{2,1,0:T(8,128)S(1)} %fusion.13), kind=kOutput, calls=%fused_computation.11 | convolution fusion | flops 6443499520 | bytes 10485764 | tf_op jit(solution)/shard_map/dot_general | solution.py:68
  123.6 13.1 %gather_fusion.1 = bf16[2048]{0:T(1024)(128)(2,1)S(1)} fusion(bf16[2049]{0:T(1024)(128)(2,1)S(1)} %pad_maximum_fusion, s32[2048]{0:T(1024)S(1)} %fusion.5), kind=kCustom, calls=%fused_computation.1 | custom fusion | bytes 16384 | tf_op jit(solution)/shard_map/gather | solution.py:47
  137.4 6.4 %all-to-all-start.1 = ((bf16[2,16,64]{2,0,1:T(2,128)(2,1)}), bf16[2,16,64]{2,0,1:T(2,128)(2,1)S(1)}, u32[]{:S(2)}, u32[]{:S(2)}) async-start(bf16[2,16,64]{2,0,1:T(2,128)(2,1)} %copy.20), calls=%async_computation.1 | async-start | bytes 16384 | tf_op jit(solution)/shard_map/all_to_all | solution.py:50
  143.9 5.0 %all-to-all-done.1 = bf16[2,16,64]{2,0,1:T(2,128)(2,1)S(1)} async-done(((bf16[2,16,64]{2,0,1:T(2,128)(2,1)}), bf16[2,16,64]{2,0,1:T(2,128)(2,1)S(1)}, u32[]{:S(2)}, u32[]{:S(2)}) %all-to-all-start.1) | async-done | bytes 4128 | tf_op jit(solution)/shard_map/all_to_all | solution.py:50
  149.4 3.1 all-gather
  152.5 10.1 %multiply_subtract_fusion = f32[512,1024]{1,0:T(8,128)S(1)} fusion(f32[1024,1024]{1,0:T(8,128)} %convert_add_fusion, s32[]{:T(128)S(6)} %select_n.38, f32[2,512,1024]{2,1,0:T(8,128)} %copy-done.4), kind=kOutput, calls=%fused_computation.10 | convolution fusion | flops 6443499520 | bytes 10485764 | tf_op jit(solution)/shard_map/dot_general | solution.py:68
  164.0 1.9 fusion.8
  165.9 9.7 %fusion.14 = f32[512,1024]{1,0:T(8,128)S(1)} fusion(f32[512,1024]{1,0:T(8,128)} %copy-done.1, f32[1024,1024]{1,0:T(8,128)} %all-gather.11.cloned.1.call-done), kind=kOutput, calls=%fused_computation.40 | convolution fusion | flops 6442450944 | bytes 8388608 | tf_op jit(solution)/shard_map/dot_general | solution.py:18
  175.6 163.7 %while.12 = (s32[]{:T(128)}, f32[512]{0:T(512)S(1)}, pred[]{:T(512)}, f32[512,1024]{1,0:T(8,128)S(1)}, f32[512]{0:T(512)S(1)}, /*index=5*/f32[512]{0:T(512)S(1)}, s32[]{:T(128)}) while((s32[]{:T(128)}, f32[512]{0:T(512)S(1)}, pred[]{:T(512)}, f32[512,1024]{1,0:T(8,128)S(1)}, f32[512]{0:T(512)S(1)}, /*index=5*/f32[512]{0:T(512)S(1)}, ...), condition=%wide.region_5.6_spmd, body=%wide.region_4.5_spmd.sunk | while | flops 6292482 | bytes 2130038 | solution.py:91
  179.3 2.2 collective-permute-start
  181.5 3.9 %collective-permute-done = f32[512]{0:T(512)S(1)} collective-permute-done((f32[512]{0:T(512)S(1)}, f32[512]{0:T(512)S(1)}, u32[]{:S(2)}, u32[]{:S(2)}) %collective-permute-start) | collective-permute-done | bytes 2080 | tf_op jit(solution)/shard_map/while/body/eval_jaxpr/ppermute | solution.py:14
  185.4 3.0 all-gather.5
  190.3 1.9 collective-permute-start
  192.2 4.2 %collective-permute-done = f32[512]{0:T(512)S(1)} collective-permute-done((f32[512]{0:T(512)S(1)}, f32[512]{0:T(512)S(1)}, u32[]{:S(2)}, u32[]{:S(2)}) %collective-permute-start) | collective-permute-done | bytes 2080 | tf_op jit(solution)/shard_map/while/body/eval_jaxpr/ppermute | solution.py:14
  196.4 3.0 all-gather.5
  201.3 1.9 collective-permute-start
  203.2 4.2 %collective-permute-done = f32[512]{0:T(512)S(1)} collective-permute-done((f32[512]{0:T(512)S(1)}, f32[512]{0:T(512)S(1)}, u32[]{:S(2)}, u32[]{:S(2)}) %collective-permute-start) | collective-permute-done | bytes 2080 | tf_op jit(solution)/shard_map/while/body/eval_jaxpr/ppermute | solution.py:14
  207.4 3.0 all-gather.5
  212.2 1.9 collective-permute-start
  214.2 4.2 %collective-permute-done = f32[512]{0:T(512)S(1)} collective-permute-done((f32[512]{0:T(512)S(1)}, f32[512]{0:T(512)S(1)}, u32[]{:S(2)}, u32[]{:S(2)}) %collective-permute-start) | collective-permute-done | bytes 2080 | tf_op jit(solution)/shard_map/while/body/eval_jaxpr/ppermute | solution.py:14
  218.4 3.0 all-gather.5
  223.2 1.9 collective-permute-start
  225.2 4.2 %collective-permute-done = f32[512]{0:T(512)S(1)} collective-permute-done((f32[512]{0:T(512)S(1)}, f32[512]{0:T(512)S(1)}, u32[]{:S(2)}, u32[]{:S(2)}) %collective-permute-start) | collective-permute-done | bytes 2080 | tf_op jit(solution)/shard_map/while/body/eval_jaxpr/ppermute | solution.py:14
  229.4 3.0 all-gather.5
  234.2 1.9 collective-permute-start
  236.2 4.2 %collective-permute-done = f32[512]{0:T(512)S(1)} collective-permute-done((f32[512]{0:T(512)S(1)}, f32[512]{0:T(512)S(1)}, u32[]{:S(2)}, u32[]{:S(2)}) %collective-permute-start) | collective-permute-done | bytes 2080 | tf_op jit(solution)/shard_map/while/body/eval_jaxpr/ppermute | solution.py:14
  240.4 3.0 all-gather.5
  245.2 1.9 collective-permute-start
  247.1 4.2 %collective-permute-done = f32[512]{0:T(512)S(1)} collective-permute-done((f32[512]{0:T(512)S(1)}, f32[512]{0:T(512)S(1)}, u32[]{:S(2)}, u32[]{:S(2)}) %collective-permute-start) | collective-permute-done | bytes 2080 | tf_op jit(solution)/shard_map/while/body/eval_jaxpr/ppermute | solution.py:14
  251.3 3.0 all-gather.5
  256.2 1.9 collective-permute-start
  258.1 4.2 %collective-permute-done = f32[512]{0:T(512)S(1)} collective-permute-done((f32[512]{0:T(512)S(1)}, f32[512]{0:T(512)S(1)}, u32[]{:S(2)}, u32[]{:S(2)}) %collective-permute-start) | collective-permute-done | bytes 2080 | tf_op jit(solution)/shard_map/while/body/eval_jaxpr/ppermute | solution.py:14
  262.3 3.0 all-gather.5
  267.2 1.9 collective-permute-start
  269.1 4.2 %collective-permute-done = f32[512]{0:T(512)S(1)} collective-permute-done((f32[512]{0:T(512)S(1)}, f32[512]{0:T(512)S(1)}, u32[]{:S(2)}, u32[]{:S(2)}) %collective-permute-start) | collective-permute-done | bytes 2080 | tf_op jit(solution)/shard_map/while/body/eval_jaxpr/ppermute | solution.py:14
  273.3 3.0 all-gather.5
  278.2 1.9 collective-permute-start
  280.1 4.2 %collective-permute-done = f32[512]{0:T(512)S(1)} collective-permute-done((f32[512]{0:T(512)S(1)}, f32[512]{0:T(512)S(1)}, u32[]{:S(2)}, u32[]{:S(2)}) %collective-permute-start) | collective-permute-done | bytes 2080 | tf_op jit(solution)/shard_map/while/body/eval_jaxpr/ppermute | solution.py:14
  284.3 3.0 all-gather.5
  289.1 1.9 collective-permute-start
  291.1 4.2 %collective-permute-done = f32[512]{0:T(512)S(1)} collective-permute-done((f32[512]{0:T(512)S(1)}, f32[512]{0:T(512)S(1)}, u32[]{:S(2)}, u32[]{:S(2)}) %collective-permute-start) | collective-permute-done | bytes 2080 | tf_op jit(solution)/shard_map/while/body/eval_jaxpr/ppermute | solution.py:14
  295.3 3.0 all-gather.5
  300.1 1.9 collective-permute-start
  302.1 4.2 %collective-permute-done = f32[512]{0:T(512)S(1)} collective-permute-done((f32[512]{0:T(512)S(1)}, f32[512]{0:T(512)S(1)}, u32[]{:S(2)}, u32[]{:S(2)}) %collective-permute-start) | collective-permute-done | bytes 2080 | tf_op jit(solution)/shard_map/while/body/eval_jaxpr/ppermute | solution.py:14
  306.3 3.0 all-gather.5
  311.1 1.9 collective-permute-start
  313.1 4.2 %collective-permute-done = f32[512]{0:T(512)S(1)} collective-permute-done((f32[512]{0:T(512)S(1)}, f32[512]{0:T(512)S(1)}, u32[]{:S(2)}, u32[]{:S(2)}) %collective-permute-start) | collective-permute-done | bytes 2080 | tf_op jit(solution)/shard_map/while/body/eval_jaxpr/ppermute | solution.py:14
  317.3 3.0 all-gather.5
  322.1 1.9 collective-permute-start
  324.0 4.2 %collective-permute-done = f32[512]{0:T(512)S(1)} collective-permute-done((f32[512]{0:T(512)S(1)}, f32[512]{0:T(512)S(1)}, u32[]{:S(2)}, u32[]{:S(2)}) %collective-permute-start) | collective-permute-done | bytes 2080 | tf_op jit(solution)/shard_map/while/body/eval_jaxpr/ppermute | solution.py:14
  328.2 3.0 all-gather.5
  333.1 1.9 collective-permute-start
  335.0 4.2 %collective-permute-done = f32[512]{0:T(512)S(1)} collective-permute-done((f32[512]{0:T(512)S(1)}, f32[512]{0:T(512)S(1)}, u32[]{:S(2)}, u32[]{:S(2)}) %collective-permute-start) | collective-permute-done | bytes 2080 | tf_op jit(solution)/shard_map/while/body/eval_jaxpr/ppermute | solution.py:14
  339.2 3.1 all-gather.2
  342.3 3.4 fusion.16
  347.6 1.9 fusion.17
  (93 shorter events, 42.6 us)
Async XLA Ops:
  6.5 10.6 %copy-start.5 = (s32[2048,1]{0,1:T(1,128)S(1)}, s32[2048,1]{0,1:T(1,128)}, u32[]{:S(2)}) copy-start(s32[2048,1]{0,1:T(1,128)} %param.11) | copy-start | bytes 24580
  6.5 101.5 %all-gather.9.cloned.1.call-start = ((), (), s32[]{:S(2)}) async-start(), calls=%async_computation.2 | async-start | bytes 6291456 | tf_op jit(solution)/shard_map/all_gather | solution.py:57
  93.6 72.3 %all-gather.11.cloned.1.call-start = ((), (), s32[]{:S(2)}) async-start(), calls=%async_computation.3 | async-start | bytes 6291456 | tf_op jit(solution)/shard_map/all_gather | solution.py:77
  93.7 14.4 %copy-start.3 = (bf16[2,16,64,512]{3,2,1,0:T(8,128)(2,1)S(1)}, bf16[2,16,64,512]{3,2,1,0:T(8,128)(2,1)}, u32[]{:S(2)}) copy-start(bf16[2,16,64,512]{3,2,1,0:T(8,128)(2,1)} %copy.18) | copy-start | bytes 6291460
  108.0 6.7 %copy-start = (f32[1024,1024]{1,0:T(8,128)S(1)}, f32[1024,1024]{1,0:T(8,128)}, u32[]{:S(2)}) copy-start(f32[1024,1024]{1,0:T(8,128)} %convert_add_fusion) | copy-start | bytes 12582916
  112.7 2.0 copy-start.4
  123.0 0.7 copy-start.6
  123.6 20.2 %copy-start.7 = (f32[1024]{0:T(1024)S(1)}, f32[1024]{0:T(1024)}, u32[]{:S(2)}) copy-start(f32[1024]{0:T(1024)} %param.7) | copy-start | bytes 12292
  137.4 11.5 %all-to-all-start.1 = ((bf16[2,16,64]{2,0,1:T(2,128)(2,1)}), bf16[2,16,64]{2,0,1:T(2,128)(2,1)S(1)}, u32[]{:S(2)}, u32[]{:S(2)}) async-start(bf16[2,16,64]{2,0,1:T(2,128)(2,1)} %copy.20), calls=%async_computation.1 | async-start | bytes 16384 | tf_op jit(solution)/shard_map/all_to_all | solution.py:50
  162.7 1.3 copy-start.1
  179.3 6.1 %collective-permute-start = (f32[512]{0:T(512)S(1)}, f32[512]{0:T(512)S(1)}, u32[]{:S(2)}, u32[]{:S(2)}) collective-permute-start(f32[512]{0:T(512)S(1)} %add.85), channel_id=1, source_target_pairs={{0,2},{2,4},{4,6},{6,8},{8,10},{10,12},{12,14},{14,16},{16,18},{18... | collective-permute-start | bytes 6152 | tf_op jit(solution)/shard_map/while/body/eval_jaxpr/ppermute | solution.py:14
  190.3 6.1 %collective-permute-start = (f32[512]{0:T(512)S(1)}, f32[512]{0:T(512)S(1)}, u32[]{:S(2)}, u32[]{:S(2)}) collective-permute-start(f32[512]{0:T(512)S(1)} %add.85), channel_id=1, source_target_pairs={{0,2},{2,4},{4,6},{6,8},{8,10},{10,12},{12,14},{14,16},{16,18},{18... | collective-permute-start | bytes 6152 | tf_op jit(solution)/shard_map/while/body/eval_jaxpr/ppermute | solution.py:14
  201.3 6.1 %collective-permute-start = (f32[512]{0:T(512)S(1)}, f32[512]{0:T(512)S(1)}, u32[]{:S(2)}, u32[]{:S(2)}) collective-permute-start(f32[512]{0:T(512)S(1)} %add.85), channel_id=1, source_target_pairs={{0,2},{2,4},{4,6},{6,8},{8,10},{10,12},{12,14},{14,16},{16,18},{18... | collective-permute-start | bytes 6152 | tf_op jit(solution)/shard_map/while/body/eval_jaxpr/ppermute | solution.py:14
  212.2 6.1 %collective-permute-start = (f32[512]{0:T(512)S(1)}, f32[512]{0:T(512)S(1)}, u32[]{:S(2)}, u32[]{:S(2)}) collective-permute-start(f32[512]{0:T(512)S(1)} %add.85), channel_id=1, source_target_pairs={{0,2},{2,4},{4,6},{6,8},{8,10},{10,12},{12,14},{14,16},{16,18},{18... | collective-permute-start | bytes 6152 | tf_op jit(solution)/shard_map/while/body/eval_jaxpr/ppermute | solution.py:14
  223.2 6.1 %collective-permute-start = (f32[512]{0:T(512)S(1)}, f32[512]{0:T(512)S(1)}, u32[]{:S(2)}, u32[]{:S(2)}) collective-permute-start(f32[512]{0:T(512)S(1)} %add.85), channel_id=1, source_target_pairs={{0,2},{2,4},{4,6},{6,8},{8,10},{10,12},{12,14},{14,16},{16,18},{18... | collective-permute-start | bytes 6152 | tf_op jit(solution)/shard_map/while/body/eval_jaxpr/ppermute | solution.py:14
  234.2 6.1 %collective-permute-start = (f32[512]{0:T(512)S(1)}, f32[512]{0:T(512)S(1)}, u32[]{:S(2)}, u32[]{:S(2)}) collective-permute-start(f32[512]{0:T(512)S(1)} %add.85), channel_id=1, source_target_pairs={{0,2},{2,4},{4,6},{6,8},{8,10},{10,12},{12,14},{14,16},{16,18},{18... | collective-permute-start | bytes 6152 | tf_op jit(solution)/shard_map/while/body/eval_jaxpr/ppermute | solution.py:14
  245.2 6.1 %collective-permute-start = (f32[512]{0:T(512)S(1)}, f32[512]{0:T(512)S(1)}, u32[]{:S(2)}, u32[]{:S(2)}) collective-permute-start(f32[512]{0:T(512)S(1)} %add.85), channel_id=1, source_target_pairs={{0,2},{2,4},{4,6},{6,8},{8,10},{10,12},{12,14},{14,16},{16,18},{18... | collective-permute-start | bytes 6152 | tf_op jit(solution)/shard_map/while/body/eval_jaxpr/ppermute | solution.py:14
  256.2 6.1 %collective-permute-start = (f32[512]{0:T(512)S(1)}, f32[512]{0:T(512)S(1)}, u32[]{:S(2)}, u32[]{:S(2)}) collective-permute-start(f32[512]{0:T(512)S(1)} %add.85), channel_id=1, source_target_pairs={{0,2},{2,4},{4,6},{6,8},{8,10},{10,12},{12,14},{14,16},{16,18},{18... | collective-permute-start | bytes 6152 | tf_op jit(solution)/shard_map/while/body/eval_jaxpr/ppermute | solution.py:14
  267.2 6.1 %collective-permute-start = (f32[512]{0:T(512)S(1)}, f32[512]{0:T(512)S(1)}, u32[]{:S(2)}, u32[]{:S(2)}) collective-permute-start(f32[512]{0:T(512)S(1)} %add.85), channel_id=1, source_target_pairs={{0,2},{2,4},{4,6},{6,8},{8,10},{10,12},{12,14},{14,16},{16,18},{18... | collective-permute-start | bytes 6152 | tf_op jit(solution)/shard_map/while/body/eval_jaxpr/ppermute | solution.py:14
  278.2 6.1 %collective-permute-start = (f32[512]{0:T(512)S(1)}, f32[512]{0:T(512)S(1)}, u32[]{:S(2)}, u32[]{:S(2)}) collective-permute-start(f32[512]{0:T(512)S(1)} %add.85), channel_id=1, source_target_pairs={{0,2},{2,4},{4,6},{6,8},{8,10},{10,12},{12,14},{14,16},{16,18},{18... | collective-permute-start | bytes 6152 | tf_op jit(solution)/shard_map/while/body/eval_jaxpr/ppermute | solution.py:14
  289.1 6.1 %collective-permute-start = (f32[512]{0:T(512)S(1)}, f32[512]{0:T(512)S(1)}, u32[]{:S(2)}, u32[]{:S(2)}) collective-permute-start(f32[512]{0:T(512)S(1)} %add.85), channel_id=1, source_target_pairs={{0,2},{2,4},{4,6},{6,8},{8,10},{10,12},{12,14},{14,16},{16,18},{18... | collective-permute-start | bytes 6152 | tf_op jit(solution)/shard_map/while/body/eval_jaxpr/ppermute | solution.py:14
  300.1 6.1 %collective-permute-start = (f32[512]{0:T(512)S(1)}, f32[512]{0:T(512)S(1)}, u32[]{:S(2)}, u32[]{:S(2)}) collective-permute-start(f32[512]{0:T(512)S(1)} %add.85), channel_id=1, source_target_pairs={{0,2},{2,4},{4,6},{6,8},{8,10},{10,12},{12,14},{14,16},{16,18},{18... | collective-permute-start | bytes 6152 | tf_op jit(solution)/shard_map/while/body/eval_jaxpr/ppermute | solution.py:14
  311.1 6.1 %collective-permute-start = (f32[512]{0:T(512)S(1)}, f32[512]{0:T(512)S(1)}, u32[]{:S(2)}, u32[]{:S(2)}) collective-permute-start(f32[512]{0:T(512)S(1)} %add.85), channel_id=1, source_target_pairs={{0,2},{2,4},{4,6},{6,8},{8,10},{10,12},{12,14},{14,16},{16,18},{18... | collective-permute-start | bytes 6152 | tf_op jit(solution)/shard_map/while/body/eval_jaxpr/ppermute | solution.py:14
  322.1 6.1 %collective-permute-start = (f32[512]{0:T(512)S(1)}, f32[512]{0:T(512)S(1)}, u32[]{:S(2)}, u32[]{:S(2)}) collective-permute-start(f32[512]{0:T(512)S(1)} %add.85), channel_id=1, source_target_pairs={{0,2},{2,4},{4,6},{6,8},{8,10},{10,12},{12,14},{14,16},{16,18},{18... | collective-permute-start | bytes 6152 | tf_op jit(solution)/shard_map/while/body/eval_jaxpr/ppermute | solution.py:14
  333.1 6.1 %collective-permute-start = (f32[512]{0:T(512)S(1)}, f32[512]{0:T(512)S(1)}, u32[]{:S(2)}, u32[]{:S(2)}) collective-permute-start(f32[512]{0:T(512)S(1)} %add.85), channel_id=1, source_target_pairs={{0,2},{2,4},{4,6},{6,8},{8,10},{10,12},{12,14},{14,16},{16,18},{18... | collective-permute-start | bytes 6152 | tf_op jit(solution)/shard_map/while/body/eval_jaxpr/ppermute | solution.py:14
  339.2 8.4 %copy-start.2 = (f32[512,1024]{1,0:T(8,128)S(1)}, f32[512,1024]{1,0:T(8,128)}, u32[]{:S(2)}) copy-start(f32[512,1024]{1,0:T(8,128)} %copy-done.1) | copy-start | bytes 6291460
Sparse Core Ops, SparseCore 0:
  93.7 14.2 all-gather.8
  123.1 14.8 all-gather.10
where the time goes:
time: 358 us; the launch traced here: 357 us
  blocking collectives  105 us (29%)
  waiting for transfers between devices  77.1 us (22%)
  matrix products  68.2 us (19%)
  local copies, waits for them, and re-layouts  40.7 us (11%)
  starting transfers between devices  35.6 us (10%)
  other arithmetic  16.2 us (5%)
  between operations  13.6 us (4%)
    ppermute x15, waiting for transfers between devices, shifted(): lax.ppermute(value, axis, [(source, source + steps) for source in range(f...  62.7 us
    all_to_all x1, blocking collectives, body(): lax.all_to_all(send_rows, 'tm', split_axis=1, concat_axis=1, tiled=True)  53.8 us
    all_gather x15, blocking collectives, advance(): whole_state = lax.all_gather(state_rows, 'row', axis=0, tiled=True)  43.5 us
    ppermute x15, starting transfers between devices, shifted(): lax.ppermute(value, axis, [(source, source + steps) for source in range(f...  29.1 us
    dot_general x15, matrix products, advance(): jnp.dot(composed, whole_state, precision=lax.Precision.HIGHEST)  28 us
    dot_general x2, matrix products, body(): jnp.dot(information[slab_index], evolve, precision=lax.Precision.HIGHEST)  18.4 us
    gather x1, local copies, waits for them, and re-layouts, body(): padded_values[slot_table].reshape(SLAB_DEV, time_devs, capacity)  13.1 us
    dot_general x1, matrix products, left_product(): new_matrix = jnp.dot(left_rows, pieces[0], precision=lax.Precision.HIGHEST)  9.65 us
  transfers between devices with their start and end apart: 18, of which 17 were waited for; matrix products, arithmetic and copies ran while one was open for 9% of the time, Pallas kernels for 0%

commit v1 on v0

--- a/solution.py
+++ b/solution.py
@@ -83,7 +83,10 @@
     initial_rows = lax.dynamic_slice_in_dim(initial, row_start, local_cols, 0)
 
     def advance(turn, state_rows):
-        whole_state = lax.all_gather(state_rows, "row", axis=0, tiled=True)
+        found = []
+        for _ in range(lax.axis_size("row")):
+            found.append(state_rows)
+        whole_state = jnp.concatenate(lax.all_to_all(jnp.stack(found), "row", 0, 0), axis=0)
         leaving = jnp.dot(composed, whole_state, precision=lax.Precision.HIGHEST) + composed_offset
         arriving = shifted(leaving, "tm", 1)
         return jnp.where(time_index == 0, initial_rows, arriving)

time: 358 us -> 386 us (1.078)
  blocking collectives: 105 us -> 134 us
    all_to_all x0 -> x15, blocking collectives: none -> 71.6 us  [advance(): lax.all_to_all(jnp.stack(found), 'row', 0, 0)]
    all_gather x15 -> x0, blocking collectives: 43.5 us -> none  [advance(): whole_state = lax.all_gather(state_rows, 'row', axis=0, tiled=True)]
    another operation x2 -> x17, other arithmetic: 9.27 us -> 9.44 us
  transfers between devices with their start and end apart: 18 -> 18, of which waited for: 17 -> 17; matrix products, arithmetic and copies ran while one was open for 9% -> 8% of each run, Pallas kernels for 0% -> 0%
where the time goes in v1:
time: 386 us; the launch traced here: 385 us
  blocking collectives  134 us (35%)
  waiting for transfers between devices  77.1 us (20%)
  matrix products  67.5 us (17%)
  local copies, waits for them, and re-layouts  40.8 us (11%)
  starting transfers between devices  35.6 us (9%)
  other arithmetic  16.3 us (4%)
  between operations  13.6 us (4%)
    all_to_all x15, blocking collectives, advance(): lax.all_to_all(jnp.stack(found), 'row', 0, 0)  71.6 us
    ppermute x15, waiting for transfers between devices, shifted(): lax.ppermute(value, axis, [(source, source + steps) for source in range(f...  62.7 us
    all_to_all x1, blocking collectives, body(): lax.all_to_all(send_rows, 'tm', split_axis=1, concat_axis=1, tiled=True)  53.8 us
    ppermute x15, starting transfers between devices, shifted(): lax.ppermute(value, axis, [(source, source + steps) for source in range(f...  29.1 us
    dot_general x15, matrix products, advance(): jnp.dot(composed, whole_state, precision=lax.Precision.HIGHEST)  27.2 us
    dot_general x2, matrix products, body(): jnp.dot(information[slab_index], evolve, precision=lax.Precision.HIGHEST)  18.4 us
    gather x1, local copies, waits for them, and re-layouts, body(): padded_values[slot_table].reshape(SLAB_DEV, time_devs, capacity)  13.1 us
    dot_general x1, matrix products, left_product(): new_matrix = jnp.dot(left_rows, pieces[0], precision=lax.Precision.HIGHEST)  9.65 us
  transfers between devices with their start and end apart: 18, of which 17 were waited for; matrix products, arithmetic and copies ran while one was open for 8% of the time, Pallas kernels for 0%

profile of v1, /device:TPU:9, one launch (start us, length us, event | category | flops | bytes accessed | tf_op | source)
XLA Modules:
  0.0 384.6 jit_solution(9978014133052833046)
XLA Ops:
  7.3 9.1 %reduce-window.6 = s32[32,16,128]{2,1,0:T(8,128)S(1)} reduce-window(s32[32,16,128]{2,1,0:T(8,128)S(1)} %fusion.4, s32[]{:T(128)} %copy.37), window={size=1x1x128 pad=0_0x0_0x127_0}, to_apply=%region_0.0 | reduce-window | flops 8323072 | bytes 524292 | tf_op jit(solution)/shard_map/reduce-window
  17.3 8.0 %scatter_custom_fusion = s32[2048]{0:T(1024)S(1)} fusion(s32[2048]{0:T(1024)S(1)} %bitcast.110, s32[2048]{0:T(1024)S(1)} %iota.23, s32[]{:T(128)} %constant.63.clone.1), kind=kCustom, calls=%fused_computation.35 | custom fusion | bytes 8196 | tf_op jit(solution)/shard_map/scatter | solution.py:42
  27.1 9.2 %gather_fusion = bf16[2048,512]{1,0:T(8,128)(2,1)} fusion(bf16[2049,512]{1,0:T(8,128)(2,1)S(1)} %concatenate.6, s32[2048]{0:T(1024)S(1)} %fusion.5), kind=kCustom, calls=%fused_computation | custom fusion | bytes 4202496 | tf_op jit(solution)/shard_map/gather | solution.py:46
  38.2 53.8 %all_to_all.23 = bf16[2,16,64,512]{3,2,0,1:T(8,128)(2,1)S(1)} all-to-all(bf16[2,16,64,512]{3,2,0,1:T(8,128)(2,1)S(1)} %copy.17), channel_id=1, replica_groups=mesh['tm'=16,'row'=2] {'tm'}, dimensions={1} | all-to-all | bytes 4194304 | tf_op jit(solution)/shard_map/all_to_all | solution.py:49
  93.7 5.0 %convert_add_fusion = f32[1024,1024]{1,0:T(8,128)} fusion(f32[1024,1024]{1,0:T(8,128)} %param.8), kind=kLoop, calls=%fused_computation.5 | loop fusion | flops 3145728 | bytes 8388608 | tf_op jit(solution)/shard_map/add | solution.py:61
  98.6 9.4 %all-gather.6.cloned.1.call-done = bf16[2,1024,1024]{2,1,0:T(8,128)(2,1)} async-done(((bf16[2,1024,512]{2,1,0:T(8,128)(2,1)}), bf16[2,1024,1024]{2,1,0:T(8,128)(2,1)}) %all-gather.6.cloned.1.call-update) | async-done | bytes 4194320 | tf_op jit(solution)/shard_map/all_gather | solution.py:57
  108.0 4.7 %fusion.13 = f32[2,512,1024]{2,1,0:T(8,128)S(1)} fusion(bf16[2,1024,512]{2,1,0:T(8,128)(2,1)S(1)} %bitcast.86, bf16[2,1024,1024]{2,1,0:T(8,128)(2,1)} %all-gather.6.cloned.1.call-done), kind=kOutput, calls=%fused_computation.40 | convolution fusion | flops 2147483648 | bytes 10485760 | tf_op jit(solution)/shard_map/sra,srb->sab/dot_general | solution.py:54
  112.8 1.9 copy-done.4
  114.7 8.2 %multiply_subtract_fusion.1 = f32[512,1024]{1,0:T(8,128)} fusion(f32[1024,1024]{1,0:T(8,128)S(1)} %copy-done, s32[]{:T(128)S(6)} %select_n.38, f32[2,512,1024]{2,1,0:T(8,128)S(1)} %fusion.13), kind=kOutput, calls=%fused_computation.12 | convolution fusion | flops 6443499520 | bytes 10485764 | tf_op jit(solution)/shard_map/dot_general | solution.py:68
  123.6 13.1 %gather_fusion.1 = bf16[2048]{0:T(1024)(128)(2,1)S(1)} fusion(bf16[2049]{0:T(1024)(128)(2,1)S(1)} %pad_maximum_fusion.1, s32[2048]{0:T(1024)S(1)} %fusion.5), kind=kCustom, calls=%fused_computation.1 | custom fusion | bytes 16384 | tf_op jit(solution)/shard_map/gather | solution.py:47
  137.4 6.4 %all-to-all-start.2 = ((bf16[2,16,64]{2,0,1:T(2,128)(2,1)}), bf16[2,16,64]{2,0,1:T(2,128)(2,1)S(1)}, u32[]{:S(2)}, u32[]{:S(2)}) async-start(bf16[2,16,64]{2,0,1:T(2,128)(2,1)} %copy.20), calls=%async_computation.2 | async-start | bytes 16384 | tf_op jit(solution)/shard_map/all_to_all | solution.py:50
  143.9 5.0 %all-to-all-done.2 = bf16[2,16,64]{2,0,1:T(2,128)(2,1)S(1)} async-done(((bf16[2,16,64]{2,0,1:T(2,128)(2,1)}), bf16[2,16,64]{2,0,1:T(2,128)(2,1)S(1)}, u32[]{:S(2)}, u32[]{:S(2)}) %all-to-all-start.2) | async-done | bytes 4128 | tf_op jit(solution)/shard_map/all_to_all | solution.py:50
  149.4 3.1 all-gather
  152.5 10.1 %multiply_subtract_fusion = f32[512,1024]{1,0:T(8,128)S(1)} fusion(f32[1024,1024]{1,0:T(8,128)} %convert_add_fusion, s32[]{:T(128)S(6)} %select_n.38, f32[2,512,1024]{2,1,0:T(8,128)} %copy-done.4), kind=kOutput, calls=%fused_computation.11 | convolution fusion | flops 6443499520 | bytes 10485764 | tf_op jit(solution)/shard_map/dot_general | solution.py:68
  165.9 9.7 %fusion.14 = f32[512,1024]{1,0:T(8,128)S(1)} fusion(f32[512,1024]{1,0:T(8,128)} %copy-done.1, f32[1024,1024]{1,0:T(8,128)} %all-gather.8.cloned.1.call-done), kind=kOutput, calls=%fused_computation.41 | convolution fusion | flops 6442450944 | bytes 8388608 | tf_op jit(solution)/shard_map/dot_general | solution.py:18
  175.6 191.3 %while.12 = (s32[]{:T(128)}, f32[512]{0:T(512)S(1)}, pred[]{:T(512)}, f32[512,1024]{1,0:T(8,128)S(1)}, f32[512]{0:T(512)S(1)}, /*index=5*/f32[512]{0:T(512)S(1)}, s32[]{:T(128)}) while((s32[]{:T(128)}, f32[512]{0:T(512)S(1)}, pred[]{:T(512)}, f32[512,1024]{1,0:T(8,128)S(1)}, f32[512]{0:T(512)S(1)}, /*index=5*/f32[512]{0:T(512)S(1)}, ...), condition=%wide.region_5.6_spmd, body=%wide.region_4.5_spmd.sunk | while | flops 6293506 | bytes 2146422 | solution.py:94
  175.6 3.7 all_to_all.24
  181.1 2.2 collective-permute-start
  183.3 3.9 %collective-permute-done = f32[512]{0:T(512)S(1)} collective-permute-done((f32[512]{0:T(512)S(1)}, f32[512]{0:T(512)S(1)}, u32[]{:S(2)}, u32[]{:S(2)}) %collective-permute-start) | collective-permute-done | bytes 2080 | tf_op jit(solution)/shard_map/while/body/eval_jaxpr/ppermute | solution.py:14
  187.3 4.8 %all_to_all.24 = f32[2,1,512]{2,1,0:T(1,128)S(1)} all-to-all(f32[2,1,512]{2,1,0:T(1,128)S(1)} %all_to_all.18), channel_id=1, replica_groups=mesh['tm'=16,'row'=2] {'row'}, dimensions={0} | all-to-all | bytes 8192 | tf_op jit(solution)/shard_map/while/body/eval_jaxpr/all_to_all | solution.py:89
  194.0 1.9 collective-permute-start
  195.9 4.2 %collective-permute-done = f32[512]{0:T(512)S(1)} collective-permute-done((f32[512]{0:T(512)S(1)}, f32[512]{0:T(512)S(1)}, u32[]{:S(2)}, u32[]{:S(2)}) %collective-permute-start) | collective-permute-done | bytes 2080 | tf_op jit(solution)/shard_map/while/body/eval_jaxpr/ppermute | solution.py:14
  200.1 4.8 %all_to_all.24 = f32[2,1,512]{2,1,0:T(1,128)S(1)} all-to-all(f32[2,1,512]{2,1,0:T(1,128)S(1)} %all_to_all.18), channel_id=1, replica_groups=mesh['tm'=16,'row'=2] {'row'}, dimensions={0} | all-to-all | bytes 8192 | tf_op jit(solution)/shard_map/while/body/eval_jaxpr/all_to_all | solution.py:89
  206.8 1.9 collective-permute-start
  208.7 4.2 %collective-permute-done = f32[512]{0:T(512)S(1)} collective-permute-done((f32[512]{0:T(512)S(1)}, f32[512]{0:T(512)S(1)}, u32[]{:S(2)}, u32[]{:S(2)}) %collective-permute-start) | collective-permute-done | bytes 2080 | tf_op jit(solution)/shard_map/while/body/eval_jaxpr/ppermute | solution.py:14
  212.9 4.8 %all_to_all.24 = f32[2,1,512]{2,1,0:T(1,128)S(1)} all-to-all(f32[2,1,512]{2,1,0:T(1,128)S(1)} %all_to_all.18), channel_id=1, replica_groups=mesh['tm'=16,'row'=2] {'row'}, dimensions={0} | all-to-all | bytes 8192 | tf_op jit(solution)/shard_map/while/body/eval_jaxpr/all_to_all | solution.py:89
  219.6 1.9 collective-permute-start
  221.5 4.2 %collective-permute-done = f32[512]{0:T(512)S(1)} collective-permute-done((f32[512]{0:T(512)S(1)}, f32[512]{0:T(512)S(1)}, u32[]{:S(2)}, u32[]{:S(2)}) %collective-permute-start) | collective-permute-done | bytes 2080 | tf_op jit(solution)/shard_map/while/body/eval_jaxpr/ppermute | solution.py:14
  225.8 4.8 %all_to_all.24 = f32[2,1,512]{2,1,0:T(1,128)S(1)} all-to-all(f32[2,1,512]{2,1,0:T(1,128)S(1)} %all_to_all.18), channel_id=1, replica_groups=mesh['tm'=16,'row'=2] {'row'}, dimensions={0} | all-to-all | bytes 8192 | tf_op jit(solution)/shard_map/while/body/eval_jaxpr/all_to_all | solution.py:89
  232.4 1.9 collective-permute-start
  234.4 4.2 %collective-permute-done = f32[512]{0:T(512)S(1)} collective-permute-done((f32[512]{0:T(512)S(1)}, f32[512]{0:T(512)S(1)}, u32[]{:S(2)}, u32[]{:S(2)}) %collective-permute-start) | collective-permute-done | bytes 2080 | tf_op jit(solution)/shard_map/while/body/eval_jaxpr/ppermute | solution.py:14
  238.6 4.8 %all_to_all.24 = f32[2,1,512]{2,1,0:T(1,128)S(1)} all-to-all(f32[2,1,512]{2,1,0:T(1,128)S(1)} %all_to_all.18), channel_id=1, replica_groups=mesh['tm'=16,'row'=2] {'row'}, dimensions={0} | all-to-all | bytes 8192 | tf_op jit(solution)/shard_map/while/body/eval_jaxpr/all_to_all | solution.py:89
  245.3 1.9 collective-permute-start
  247.2 4.2 %collective-permute-done = f32[512]{0:T(512)S(1)} collective-permute-done((f32[512]{0:T(512)S(1)}, f32[512]{0:T(512)S(1)}, u32[]{:S(2)}, u32[]{:S(2)}) %collective-permute-start) | collective-permute-done | bytes 2080 | tf_op jit(solution)/shard_map/while/body/eval_jaxpr/ppermute | solution.py:14
  251.4 4.8 %all_to_all.24 = f32[2,1,512]{2,1,0:T(1,128)S(1)} all-to-all(f32[2,1,512]{2,1,0:T(1,128)S(1)} %all_to_all.18), channel_id=1, replica_groups=mesh['tm'=16,'row'=2] {'row'}, dimensions={0} | all-to-all | bytes 8192 | tf_op jit(solution)/shard_map/while/body/eval_jaxpr/all_to_all | solution.py:89
  258.1 1.9 collective-permute-start
  260.0 4.2 %collective-permute-done = f32[512]{0:T(512)S(1)} collective-permute-done((f32[512]{0:T(512)S(1)}, f32[512]{0:T(512)S(1)}, u32[]{:S(2)}, u32[]{:S(2)}) %collective-permute-start) | collective-permute-done | bytes 2080 | tf_op jit(solution)/shard_map/while/body/eval_jaxpr/ppermute | solution.py:14
  264.3 4.8 %all_to_all.24 = f32[2,1,512]{2,1,0:T(1,128)S(1)} all-to-all(f32[2,1,512]{2,1,0:T(1,128)S(1)} %all_to_all.18), channel_id=1, replica_groups=mesh['tm'=16,'row'=2] {'row'}, dimensions={0} | all-to-all | bytes 8192 | tf_op jit(solution)/shard_map/while/body/eval_jaxpr/all_to_all | solution.py:89
  270.9 1.9 collective-permute-start
  272.9 4.2 %collective-permute-done = f32[512]{0:T(512)S(1)} collective-permute-done((f32[512]{0:T(512)S(1)}, f32[512]{0:T(512)S(1)}, u32[]{:S(2)}, u32[]{:S(2)}) %collective-permute-start) | collective-permute-done | bytes 2080 | tf_op jit(solution)/shard_map/while/body/eval_jaxpr/ppermute | solution.py:14
  277.1 4.8 %all_to_all.24 = f32[2,1,512]{2,1,0:T(1,128)S(1)} all-to-all(f32[2,1,512]{2,1,0:T(1,128)S(1)} %all_to_all.18), channel_id=1, replica_groups=mesh['tm'=16,'row'=2] {'row'}, dimensions={0} | all-to-all | bytes 8192 | tf_op jit(solution)/shard_map/while/body/eval_jaxpr/all_to_all | solution.py:89
  283.8 1.9 collective-permute-start
  285.7 4.2 %collective-permute-done = f32[512]{0:T(512)S(1)} collective-permute-done((f32[512]{0:T(512)S(1)}, f32[512]{0:T(512)S(1)}, u32[]{:S(2)}, u32[]{:S(2)}) %collective-permute-start) | collective-permute-done | bytes 2080 | tf_op jit(solution)/shard_map/while/body/eval_jaxpr/ppermute | solution.py:14
  289.9 4.8 %all_to_all.24 = f32[2,1,512]{2,1,0:T(1,128)S(1)} all-to-all(f32[2,1,512]{2,1,0:T(1,128)S(1)} %all_to_all.18), channel_id=1, replica_groups=mesh['tm'=16,'row'=2] {'row'}, dimensions={0} | all-to-all | bytes 8192 | tf_op jit(solution)/shard_map/while/body/eval_jaxpr/all_to_all | solution.py:89
  296.6 1.9 collective-permute-start
  298.5 4.2 %collective-permute-done = f32[512]{0:T(512)S(1)} collective-permute-done((f32[512]{0:T(512)S(1)}, f32[512]{0:T(512)S(1)}, u32[]{:S(2)}, u32[]{:S(2)}) %collective-permute-start) | collective-permute-done | bytes 2080 | tf_op jit(solution)/shard_map/while/body/eval_jaxpr/ppermute | solution.py:14
  302.8 4.8 %all_to_all.24 = f32[2,1,512]{2,1,0:T(1,128)S(1)} all-to-all(f32[2,1,512]{2,1,0:T(1,128)S(1)} %all_to_all.18), channel_id=1, replica_groups=mesh['tm'=16,'row'=2] {'row'}, dimensions={0} | all-to-all | bytes 8192 | tf_op jit(solution)/shard_map/while/body/eval_jaxpr/all_to_all | solution.py:89
  309.4 1.9 collective-permute-start
  311.4 4.2 %collective-permute-done = f32[512]{0:T(512)S(1)} collective-permute-done((f32[512]{0:T(512)S(1)}, f32[512]{0:T(512)S(1)}, u32[]{:S(2)}, u32[]{:S(2)}) %collective-permute-start) | collective-permute-done | bytes 2080 | tf_op jit(solution)/shard_map/while/body/eval_jaxpr/ppermute | solution.py:14
  315.6 4.8 %all_to_all.24 = f32[2,1,512]{2,1,0:T(1,128)S(1)} all-to-all(f32[2,1,512]{2,1,0:T(1,128)S(1)} %all_to_all.18), channel_id=1, replica_groups=mesh['tm'=16,'row'=2] {'row'}, dimensions={0} | all-to-all | bytes 8192 | tf_op jit(solution)/shard_map/while/body/eval_jaxpr/all_to_all | solution.py:89
  322.3 1.9 collective-permute-start
  324.2 4.2 %collective-permute-done = f32[512]{0:T(512)S(1)} collective-permute-done((f32[512]{0:T(512)S(1)}, f32[512]{0:T(512)S(1)}, u32[]{:S(2)}, u32[]{:S(2)}) %collective-permute-start) | collective-permute-done | bytes 2080 | tf_op jit(solution)/shard_map/while/body/eval_jaxpr/ppermute | solution.py:14
  328.4 4.8 %all_to_all.24 = f32[2,1,512]{2,1,0:T(1,128)S(1)} all-to-all(f32[2,1,512]{2,1,0:T(1,128)S(1)} %all_to_all.18), channel_id=1, replica_groups=mesh['tm'=16,'row'=2] {'row'}, dimensions={0} | all-to-all | bytes 8192 | tf_op jit(solution)/shard_map/while/body/eval_jaxpr/all_to_all | solution.py:89
  335.1 1.9 collective-permute-start
  337.0 4.2 %collective-permute-done = f32[512]{0:T(512)S(1)} collective-permute-done((f32[512]{0:T(512)S(1)}, f32[512]{0:T(512)S(1)}, u32[]{:S(2)}, u32[]{:S(2)}) %collective-permute-start) | collective-permute-done | bytes 2080 | tf_op jit(solution)/shard_map/while/body/eval_jaxpr/ppermute | solution.py:14
  341.2 4.8 %all_to_all.24 = f32[2,1,512]{2,1,0:T(1,128)S(1)} all-to-all(f32[2,1,512]{2,1,0:T(1,128)S(1)} %all_to_all.18), channel_id=1, replica_groups=mesh['tm'=16,'row'=2] {'row'}, dimensions={0} | all-to-all | bytes 8192 | tf_op jit(solution)/shard_map/while/body/eval_jaxpr/all_to_all | solution.py:89
  347.9 1.9 collective-permute-start
  349.8 4.2 %collective-permute-done = f32[512]{0:T(512)S(1)} collective-permute-done((f32[512]{0:T(512)S(1)}, f32[512]{0:T(512)S(1)}, u32[]{:S(2)}, u32[]{:S(2)}) %collective-permute-start) | collective-permute-done | bytes 2080 | tf_op jit(solution)/shard_map/while/body/eval_jaxpr/ppermute | solution.py:14
  354.1 4.8 %all_to_all.24 = f32[2,1,512]{2,1,0:T(1,128)S(1)} all-to-all(f32[2,1,512]{2,1,0:T(1,128)S(1)} %all_to_all.18), channel_id=1, replica_groups=mesh['tm'=16,'row'=2] {'row'}, dimensions={0} | all-to-all | bytes 8192 | tf_op jit(solution)/shard_map/while/body/eval_jaxpr/all_to_all | solution.py:89
  360.7 1.9 collective-permute-start
  362.7 4.2 %collective-permute-done = f32[512]{0:T(512)S(1)} collective-permute-done((f32[512]{0:T(512)S(1)}, f32[512]{0:T(512)S(1)}, u32[]{:S(2)}, u32[]{:S(2)}) %collective-permute-start) | collective-permute-done | bytes 2080 | tf_op jit(solution)/shard_map/while/body/eval_jaxpr/ppermute | solution.py:14
  366.9 3.1 all-gather.1
  370.0 3.4 fusion.16
  375.3 1.9 fusion.17
  (123 shorter events, 42.2 us)
Async XLA Ops:
  6.5 10.6 %copy-start.5 = (s32[2048,1]{0,1:T(1,128)S(1)}, s32[2048,1]{0,1:T(1,128)}, u32[]{:S(2)}) copy-start(s32[2048,1]{0,1:T(1,128)} %param.11) | copy-start | bytes 24580
  6.5 101.5 %all-gather.6.cloned.1.call-start = ((), (), s32[]{:S(2)}) async-start(), calls=%async_computation.3 | async-start | bytes 6291456 | tf_op jit(solution)/shard_map/all_gather | solution.py:57
  93.6 72.3 %all-gather.8.cloned.1.call-start = ((), (), s32[]{:S(2)}) async-start(), calls=%async_computation.4 | async-start | bytes 6291456 | tf_op jit(solution)/shard_map/all_gather | solution.py:77
  93.7 14.4 %copy-start.3 = (bf16[2,16,64,512]{3,2,1,0:T(8,128)(2,1)S(1)}, bf16[2,16,64,512]{3,2,1,0:T(8,128)(2,1)}, u32[]{:S(2)}) copy-start(bf16[2,16,64,512]{3,2,1,0:T(8,128)(2,1)} %copy.18) | copy-start | bytes 6291460
  108.0 6.7 %copy-start = (f32[1024,1024]{1,0:T(8,128)S(1)}, f32[1024,1024]{1,0:T(8,128)}, u32[]{:S(2)}) copy-start(f32[1024,1024]{1,0:T(8,128)} %convert_add_fusion) | copy-start | bytes 12582916
  112.7 2.0 copy-start.4
  123.0 0.7 copy-start.6
  123.6 20.2 %copy-start.7 = (f32[1024]{0:T(1024)S(1)}, f32[1024]{0:T(1024)}, u32[]{:S(2)}) copy-start(f32[1024]{0:T(1024)} %param.7) | copy-start | bytes 12292
  137.4 11.5 %all-to-all-start.2 = ((bf16[2,16,64]{2,0,1:T(2,128)(2,1)}), bf16[2,16,64]{2,0,1:T(2,128)(2,1)S(1)}, u32[]{:S(2)}, u32[]{:S(2)}) async-start(bf16[2,16,64]{2,0,1:T(2,128)(2,1)} %copy.20), calls=%async_computation.2 | async-start | bytes 16384 | tf_op jit(solution)/shard_map/all_to_all | solution.py:50
  162.7 1.3 copy-start.1
  181.1 6.1 %collective-permute-start = (f32[512]{0:T(512)S(1)}, f32[512]{0:T(512)S(1)}, u32[]{:S(2)}, u32[]{:S(2)}) collective-permute-start(f32[512]{0:T(512)S(1)} %add.85), channel_id=1, source_target_pairs={{0,2},{2,4},{4,6},{6,8},{8,10},{10,12},{12,14},{14,16},{16,18},{18... | collective-permute-start | bytes 6152 | tf_op jit(solution)/shard_map/while/body/eval_jaxpr/ppermute | solution.py:14
  194.0 6.1 %collective-permute-start = (f32[512]{0:T(512)S(1)}, f32[512]{0:T(512)S(1)}, u32[]{:S(2)}, u32[]{:S(2)}) collective-permute-start(f32[512]{0:T(512)S(1)} %add.85), channel_id=1, source_target_pairs={{0,2},{2,4},{4,6},{6,8},{8,10},{10,12},{12,14},{14,16},{16,18},{18... | collective-permute-start | bytes 6152 | tf_op jit(solution)/shard_map/while/body/eval_jaxpr/ppermute | solution.py:14
  206.8 6.1 %collective-permute-start = (f32[512]{0:T(512)S(1)}, f32[512]{0:T(512)S(1)}, u32[]{:S(2)}, u32[]{:S(2)}) collective-permute-start(f32[512]{0:T(512)S(1)} %add.85), channel_id=1, source_target_pairs={{0,2},{2,4},{4,6},{6,8},{8,10},{10,12},{12,14},{14,16},{16,18},{18... | collective-permute-start | bytes 6152 | tf_op jit(solution)/shard_map/while/body/eval_jaxpr/ppermute | solution.py:14
  219.6 6.1 %collective-permute-start = (f32[512]{0:T(512)S(1)}, f32[512]{0:T(512)S(1)}, u32[]{:S(2)}, u32[]{:S(2)}) collective-permute-start(f32[512]{0:T(512)S(1)} %add.85), channel_id=1, source_target_pairs={{0,2},{2,4},{4,6},{6,8},{8,10},{10,12},{12,14},{14,16},{16,18},{18... | collective-permute-start | bytes 6152 | tf_op jit(solution)/shard_map/while/body/eval_jaxpr/ppermute | solution.py:14
  232.4 6.1 %collective-permute-start = (f32[512]{0:T(512)S(1)}, f32[512]{0:T(512)S(1)}, u32[]{:S(2)}, u32[]{:S(2)}) collective-permute-start(f32[512]{0:T(512)S(1)} %add.85), channel_id=1, source_target_pairs={{0,2},{2,4},{4,6},{6,8},{8,10},{10,12},{12,14},{14,16},{16,18},{18... | collective-permute-start | bytes 6152 | tf_op jit(solution)/shard_map/while/body/eval_jaxpr/ppermute | solution.py:14
  245.3 6.1 %collective-permute-start = (f32[512]{0:T(512)S(1)}, f32[512]{0:T(512)S(1)}, u32[]{:S(2)}, u32[]{:S(2)}) collective-permute-start(f32[512]{0:T(512)S(1)} %add.85), channel_id=1, source_target_pairs={{0,2},{2,4},{4,6},{6,8},{8,10},{10,12},{12,14},{14,16},{16,18},{18... | collective-permute-start | bytes 6152 | tf_op jit(solution)/shard_map/while/body/eval_jaxpr/ppermute | solution.py:14
  258.1 6.1 %collective-permute-start = (f32[512]{0:T(512)S(1)}, f32[512]{0:T(512)S(1)}, u32[]{:S(2)}, u32[]{:S(2)}) collective-permute-start(f32[512]{0:T(512)S(1)} %add.85), channel_id=1, source_target_pairs={{0,2},{2,4},{4,6},{6,8},{8,10},{10,12},{12,14},{14,16},{16,18},{18... | collective-permute-start | bytes 6152 | tf_op jit(solution)/shard_map/while/body/eval_jaxpr/ppermute | solution.py:14
  270.9 6.1 %collective-permute-start = (f32[512]{0:T(512)S(1)}, f32[512]{0:T(512)S(1)}, u32[]{:S(2)}, u32[]{:S(2)}) collective-permute-start(f32[512]{0:T(512)S(1)} %add.85), channel_id=1, source_target_pairs={{0,2},{2,4},{4,6},{6,8},{8,10},{10,12},{12,14},{14,16},{16,18},{18... | collective-permute-start | bytes 6152 | tf_op jit(solution)/shard_map/while/body/eval_jaxpr/ppermute | solution.py:14
  283.8 6.1 %collective-permute-start = (f32[512]{0:T(512)S(1)}, f32[512]{0:T(512)S(1)}, u32[]{:S(2)}, u32[]{:S(2)}) collective-permute-start(f32[512]{0:T(512)S(1)} %add.85), channel_id=1, source_target_pairs={{0,2},{2,4},{4,6},{6,8},{8,10},{10,12},{12,14},{14,16},{16,18},{18... | collective-permute-start | bytes 6152 | tf_op jit(solution)/shard_map/while/body/eval_jaxpr/ppermute | solution.py:14
  296.6 6.1 %collective-permute-start = (f32[512]{0:T(512)S(1)}, f32[512]{0:T(512)S(1)}, u32[]{:S(2)}, u32[]{:S(2)}) collective-permute-start(f32[512]{0:T(512)S(1)} %add.85), channel_id=1, source_target_pairs={{0,2},{2,4},{4,6},{6,8},{8,10},{10,12},{12,14},{14,16},{16,18},{18... | collective-permute-start | bytes 6152 | tf_op jit(solution)/shard_map/while/body/eval_jaxpr/ppermute | solution.py:14
  309.4 6.1 %collective-permute-start = (f32[512]{0:T(512)S(1)}, f32[512]{0:T(512)S(1)}, u32[]{:S(2)}, u32[]{:S(2)}) collective-permute-start(f32[512]{0:T(512)S(1)} %add.85), channel_id=1, source_target_pairs={{0,2},{2,4},{4,6},{6,8},{8,10},{10,12},{12,14},{14,16},{16,18},{18... | collective-permute-start | bytes 6152 | tf_op jit(solution)/shard_map/while/body/eval_jaxpr/ppermute | solution.py:14
  322.3 6.1 %collective-permute-start = (f32[512]{0:T(512)S(1)}, f32[512]{0:T(512)S(1)}, u32[]{:S(2)}, u32[]{:S(2)}) collective-permute-start(f32[512]{0:T(512)S(1)} %add.85), channel_id=1, source_target_pairs={{0,2},{2,4},{4,6},{6,8},{8,10},{10,12},{12,14},{14,16},{16,18},{18... | collective-permute-start | bytes 6152 | tf_op jit(solution)/shard_map/while/body/eval_jaxpr/ppermute | solution.py:14
  335.1 6.1 %collective-permute-start = (f32[512]{0:T(512)S(1)}, f32[512]{0:T(512)S(1)}, u32[]{:S(2)}, u32[]{:S(2)}) collective-permute-start(f32[512]{0:T(512)S(1)} %add.85), channel_id=1, source_target_pairs={{0,2},{2,4},{4,6},{6,8},{8,10},{10,12},{12,14},{14,16},{16,18},{18... | collective-permute-start | bytes 6152 | tf_op jit(solution)/shard_map/while/body/eval_jaxpr/ppermute | solution.py:14
  347.9 6.1 %collective-permute-start = (f32[512]{0:T(512)S(1)}, f32[512]{0:T(512)S(1)}, u32[]{:S(2)}, u32[]{:S(2)}) collective-permute-start(f32[512]{0:T(512)S(1)} %add.85), channel_id=1, source_target_pairs={{0,2},{2,4},{4,6},{6,8},{8,10},{10,12},{12,14},{14,16},{16,18},{18... | collective-permute-start | bytes 6152 | tf_op jit(solution)/shard_map/while/body/eval_jaxpr/ppermute | solution.py:14
  360.7 6.1 %collective-permute-start = (f32[512]{0:T(512)S(1)}, f32[512]{0:T(512)S(1)}, u32[]{:S(2)}, u32[]{:S(2)}) collective-permute-start(f32[512]{0:T(512)S(1)} %add.85), channel_id=1, source_target_pairs={{0,2},{2,4},{4,6},{6,8},{8,10},{10,12},{12,14},{14,16},{16,18},{18... | collective-permute-start | bytes 6152 | tf_op jit(solution)/shard_map/while/body/eval_jaxpr/ppermute | solution.py:14
  366.9 8.4 %copy-start.2 = (f32[512,1024]{1,0:T(8,128)S(1)}, f32[512,1024]{1,0:T(8,128)}, u32[]{:S(2)}) copy-start(f32[512,1024]{1,0:T(8,128)} %copy-done.1) | copy-start | bytes 6291460
Sparse Core Ops, SparseCore 0:
  93.7 14.2 all-gather.5
  123.1 14.8 all-gather.7
